TPU v7x, 32 devices: a whole 2x2x4 slice. The times are simulated.
32 devices in a mesh: groups: 2 (over x), req: 16 (over z, y, core).
Axes of the slice: x: 2, y: 2, z: 4, core: 2. Of those that a mesh axis runs over, the one named last changes fastest.
Arguments:
- queries: bfloat16 [64, 6, 4096], P(('groups', 'req')), parts along dimension 0, may hold values from -6 to 6
- keys: bfloat16 [64, 6, 4096], P(('groups', 'req')), parts along dimension 0, may hold values from -6 to 6
- values: bfloat16 [64, 6, 4096], P(('groups', 'req')), parts along dimension 0, may hold values from -6 to 6
- gates: bfloat16 [64, 6, 4096], P(('groups', 'req')), parts along dimension 0, may hold values from -6 to 6
- states: float32 [64, 32, 128, 128], P(('groups', 'req')), parts along dimension 0, may hold values from -12 to 12
- new_slot: int32 [64], P(('groups', 'req')), parts along dimension 0, may hold values from 0 to 31, as said below
- norm_gain: float32 [4096], replicated, may hold values from 0.1 to 1.9
Outputs:
- output: bfloat16 [64, 6, 4096], P(('groups', 'req')), parts along dimension 0
There are 2 independent parts, one for each index of `groups`. A program takes and returns all parts, laid end to end along the dimension named above; an argument that names none is the same for every part. Nothing has to cross between parts.
Inputs may be any that keep to these rules, and one draw needn't show every extreme that they name: `new_slot`: A permutation of the slots. On one device (its 2 slots) at most 1 request change slot, and exactly 1 do on some devices; a request that changes slot never keeps it.
All inputs are finite; a program needn't handle non-finite values.
Results may differ from a plain program's by a relative error of at most 0.001.
Values sent between devices are 32-bit elements; how exact they have to be, the bound alone decides.
A program may use at most 64 MiB of HBM per device.

v0:
```python
import functools
import math

import jax
import jax.numpy as jnp
from jax import lax
from jax.experimental import pallas as pl
from jax.experimental.pallas import tpu as pltpu
from jax.sharding import PartitionSpec as P

D_HEAD = 128
BEFORE = 3
STEPS = 6
MODEL_HEADS = 64
GROUP = STEPS - BEFORE
LEAD = 8

MESH = pl.DeviceIdType.MESH


def silu(x):
    return x / (1.0 + jnp.exp(-x))


def split(x):
    high = x.astype(jnp.bfloat16).astype(jnp.float32)
    return high, x - high


def rows_of(src, dst):
    for t in range(STEPS):
        both = src[t].astype(jnp.float32)
        for s in range(both.shape[0]):
            dst[s, t : t + 1, :] = both[s : s + 1]


def head_slope(heads):
    return jnp.exp((heads + 1.0) * (-8.0 / MODEL_HEADS * math.log(2.0)))


def kernel(
    count,
    hubs,
    slot_hbm,
    q_hbm,
    k_hbm,
    v_hbm,
    g_hbm,
    gain_hbm,
    s_hbm,
    out_ref,
    slot_ref,
    q_v,
    k_v,
    v_v,
    g_v,
    gain_v,
    s_v,
    s_pair,
    a_v,
    b_v,
    c_v,
    w_v,
    base_v,
    scale_v,
    row_v,
    early_k,
    early_v,
    piece,
    hub_in,
    hub_out,
    q_in,
    r_out,
    hub_r,
    hub_f,
    final,
    load_sem,
    state_sem,
    send_a,
    recv_a,
    send_b,
    recv_b,
    send_c,
    recv_c,
    send_d,
    recv_d,
):
    slots, heads = s_hbm.shape[0], s_hbm.shape[1]
    width = heads * D_HEAD
    per_hub = heads // hubs
    rows = GROUP * per_hub
    room = piece.shape[1]
    first = (count - hubs) // 2
    me = lax.axis_index("req")
    is_hub = (me >= first) & (me < first + hubs)
    hub_rank = jnp.clip(me - first, 0, hubs - 1)

    loads = [
        pltpu.make_async_copy(src, dst, load_sem.at[k])
        for k, (src, dst) in enumerate(
            (
                (slot_hbm, slot_ref),
                (q_hbm, q_v),
                (k_hbm, k_v),
                (v_hbm, v_v),
                (g_hbm, g_v),
                (gain_hbm, gain_v),
            )
        )
    ]
    state_loads = [
        pltpu.make_async_copy(s_hbm.at[s], s_v.at[s], state_sem.at[s]) for s in range(slots)
    ]
    loads[0].start()
    loads[1].start()

    barrier = pltpu.get_barrier_semaphore()

    def other(k):
        return lax.rem(me + k, count)

    @pl.when(is_hub)
    def _():
        def greet(k, carry):
            pl.semaphore_signal(barrier, inc=1, device_id={"req": other(k)}, device_id_type=MESH)
            return carry

        lax.fori_loop(1, count, greet, 0, unroll=5 if (count - 1) % 5 == 0 else 1)

    @pl.when(jnp.logical_not(is_hub))
    def _():
        for j in range(hubs):
            pl.semaphore_signal(barrier, inc=1, device_id={"req": first + j}, device_id_type=MESH)

    for copy in loads[2:4] + state_loads + loads[4:]:
        copy.start()

    loads[0].wait()
    moving = jnp.int32(0)
    for s in range(slots):
        moving = jnp.where(slot_ref[s] != me * slots + s, jnp.int32(s), moving)
    wanted = slot_ref[moving] // slots
    wanted_row = jnp.full((1, D_HEAD), wanted, jnp.int32).astype(jnp.float32)

    loads[1].wait()
    rows_of(q_v, a_v)
    for s in range(slots):
        a_v[s, 0:STEPS, :] = silu(a_v[s, 0:STEPS, :])
        a_v[s, STEPS:, :] = jnp.zeros((8 - STEPS, width), jnp.float32)
    for h in range(heads):
        j, hh = divmod(h, per_hub)
        piece[j, GROUP * hh : GROUP * hh + GROUP, :] = a_v[
            moving, BEFORE:STEPS, h * D_HEAD : (h + 1) * D_HEAD
        ]
    for j in range(hubs):
        piece[j, rows : rows + 1, :] = wanted_row

    @pl.when(is_hub)
    def _():
        hub_in[me] = piece[hub_rank]

    @pl.when(is_hub)
    def _():
        pl.semaphore_wait(barrier, count - 1)

    @pl.when(jnp.logical_not(is_hub))
    def _():
        pl.semaphore_wait(barrier, hubs)

    def remote(src, dst, send, recv, target):
        return pltpu.make_async_remote_copy(
            src_ref=src,
            dst_ref=dst,
            send_sem=send,
            recv_sem=recv,
            device_id={"req": target},
            device_id_type=MESH,
        )

    def arrive(dst, recv):
        pltpu.make_async_copy(dst, dst, recv).wait()

    def each_hub(act):
        for j in range(hubs):

            @pl.when(first + j != me)
            def _():
                act(j)

    def to_hub_first(j):
        return remote(
            piece.at[j, 0 : rows + 1],
            hub_in.at[me, 0 : rows + 1],
            send_a.at[j],
            recv_a.at[me],
            first + j,
        )

    def to_hub_back(j):
        return remote(
            r_out.at[j, 0:rows], hub_r.at[me, 0:rows], send_c.at[j], recv_c.at[me], first + j
        )

    def from_hub_first(i):
        return remote(
            hub_out.at[i, 0:rows], q_in.at[hub_rank, 0:rows], send_b.at[i], recv_b.at[hub_rank], i
        )

    final_at = pl.multiple_of(LEAD + room * hub_rank, 8)

    def from_hub_back(i):
        return remote(
            hub_f.at[i, 0:rows],
            final.at[pl.ds(final_at, rows)],
            send_d.at[i],
            recv_d.at[hub_rank],
            i,
        )

    far = jnp.where(me >= count // 2, 0, max(1, hubs // 2))
    for jj in range(hubs):
        far_j = lax.rem(far + jj, hubs)

        @pl.when(first + far_j != me)
        def _():
            to_hub_first(far_j).start()


    loads[2].wait()
    loads[3].wait()
    rows_of(k_v, b_v)
    rows_of(v_v, c_v)
    for s in range(slots):
        b_v[s, 0:STEPS, :] = silu(b_v[s, 0:STEPS, :])
        c_v[s, 0:STEPS, :] = silu(c_v[s, 0:STEPS, :])
        b_v[s, STEPS:, :] = jnp.zeros((8 - STEPS, width), jnp.float32)
        c_v[s, STEPS:, :] = jnp.zeros((8 - STEPS, width), jnp.float32)

    for copy in state_loads:
        copy.wait()

    def halve(h, carry):
        for s in range(slots):
            high, low = split(s_v[s, h])
            s_pair[s, h, 0:D_HEAD, :] = high.astype(jnp.bfloat16)
            s_pair[s, h, D_HEAD:, :] = low.astype(jnp.bfloat16)
        return carry

    lax.fori_loop(0, heads, halve, 0, unroll=2)

    start = me - lax.rem(me, 2) + max(count // 2 - 2, 1) + count
    own_place = lax.rem(me - start + 2 * count, count)

    def target(k):
        return lax.rem(start + k + jnp.where(k >= own_place, 1, 0), count)

    hub_unroll = 5 if (count - 1) % 5 == 0 else 1

    @pl.when(is_hub)
    def _():
        for k in range(1, count):
            e = other(k)
            arrive(hub_in.at[e, 0 : rows + 1], recv_a.at[e])

        def choose(i):
            want = hub_in[i, rows : rows + 1, :]
            chosen = hub_in[0]
            for e in range(1, count):
                chosen = jnp.where(want == float(e), hub_in[e], chosen)
            return chosen

        def hand(k, carry):
            i = target(k)
            hub_out[i] = choose(i)
            from_hub_first(i).start()
            return carry

        lax.fori_loop(0, count - 1, hand, 0, unroll=hub_unroll)
        q_in[hub_rank] = choose(me)

    piece_row = lax.broadcasted_iota(jnp.int32, (room, D_HEAD), 0)
    piece_head = jnp.zeros((room, D_HEAD), jnp.int32)
    for hh in range(1, per_hub):
        piece_head = jnp.where(piece_row >= GROUP * hh, hh, piece_head)
    piece_step = (piece_row - GROUP * piece_head).astype(jnp.float32)
    for h in range(heads):
        j, hh = divmod(h, per_hub)
        cols = slice(h * D_HEAD, (h + 1) * D_HEAD)
        for s in range(BEFORE):
            early_k[s, j, GROUP * hh : GROUP * (hh + 1), :] = jnp.broadcast_to(
                b_v[moving, s : s + 1, cols], (GROUP, D_HEAD)
            )
            early_v[s, j, GROUP * hh : GROUP * (hh + 1), :] = jnp.broadcast_to(
                c_v[moving, s : s + 1, cols], (GROUP, D_HEAD)
            )

    step = lax.broadcasted_iota(jnp.int32, (8, D_HEAD), 0)
    step_f = step.astype(jnp.float32)

    def own(h, carry):
        cols = pl.ds(pl.multiple_of(h * D_HEAD, D_HEAD), D_HEAD)
        slope = head_slope(jnp.full((8, D_HEAD), h, jnp.int32).astype(jnp.float32))
        decay_state = jnp.exp(-slope * (step_f + 1.0))
        for s in range(slots):
            a, b, c = a_v[s, :, cols], b_v[s, :, cols], c_v[s, :, cols]
            high, low = split(a)
            left = jnp.concatenate([high, low], axis=0)
            left = jnp.concatenate([left, left], axis=1).astype(jnp.bfloat16)
            both = jnp.dot(left, s_pair[s, h], preferred_element_type=jnp.float32)
            base = decay_state * (both[:8] + both[8:])
            within = jnp.zeros((8, D_HEAD), jnp.float32)
            for back in range(STEPS):
                b_back = pltpu.roll(b, back, 0) if back else b
                c_back = pltpu.roll(c, back, 0) if back else c
                mix = jnp.sum(a * b_back, axis=1, keepdims=True)
                term = mix * c_back * jnp.exp(-slope * float(back))
                late = (step >= BEFORE) & (step < STEPS)
                if back < BEFORE:
                    keep = ((step < BEFORE) & (step >= back)) | (late & (step >= BEFORE + back))
                    within = within + jnp.where(keep, term, 0.0)
                if back:
                    cross = late & (step >= back) & (step < BEFORE + back)
                    base = base + jnp.where(cross, term, 0.0)
            base_v[s, :, cols] = base
            w_v[s, :, cols] = within
        return carry

    lax.fori_loop(0, heads, own, 0, unroll=2)

    def answer(j):
        q = q_in[j]
        high, low = split(q)
        left = jnp.concatenate([high, low], axis=0)
        left = jnp.concatenate([left, left], axis=1).astype(jnp.bfloat16)
        slope = head_slope((piece_head + j * per_hub).astype(jnp.float32))
        total = jnp.zeros((room, D_HEAD), jnp.float32)
        for hh in range(per_hub):
            both = jnp.dot(
                left, s_pair[moving, j * per_hub + hh], preferred_element_type=jnp.float32
            )
            total = jnp.where(piece_head == hh, both[:room] + both[room:], total)
        total = total * jnp.exp(-slope * (piece_step + (BEFORE + 1.0)))
        for s in range(BEFORE):
            mix = jnp.sum(q * early_k[s, j], axis=1, keepdims=True)
            total = total + mix * early_v[s, j] * jnp.exp(
                -slope * (piece_step + float(BEFORE - s))
            )
        r_out[j] = total

    split_at = max(1, hubs // 2)
    turn = jnp.where(me >= count // 2, split_at, 0)
    share = max(1, hubs // 4)
    for group in [range(k, min(k + share, hubs)) for k in range(0, hubs, share)]:
        order = [lax.rem(turn + jj, hubs) for jj in group]

        def others(act):
            for j in order:

                @pl.when(first + j != me)
                def _():
                    act(j)

        others(lambda j: arrive(q_in.at[j, 0:rows], recv_b.at[j]))
        for j in order:
            answer(j)
        others(lambda j: to_hub_back(j).start())

    @pl.when(is_hub)
    def _():
        hub_r[me] = r_out[hub_rank]

    loads[4].wait()
    loads[5].wait()
    rows_of(g_v, scale_v)
    for s in range(slots):
        gate = scale_v[s, 0:STEPS, :]
        scale_v[s, 0:STEPS, :] = gain_v[...] / (1.0 + jnp.exp(-gate))
        scale_v[s, STEPS:, :] = jnp.zeros((8 - STEPS, width), jnp.float32)
    for s in range(slots):
        mixed = base_v[s] + w_v[s]
        energy = jnp.sum(mixed * mixed, axis=1, keepdims=True) * (1.0 / width)
        row = mixed * lax.rsqrt(energy + 1e-06) * scale_v[s]
        for t in range(STEPS):
            row_v[t, s : s + 1, :] = row[t : t + 1]
    for t in range(BEFORE):
        out_ref[t] = row_v[t].astype(out_ref.dtype)

    @pl.when(is_hub)
    def _():
        for k in range(1, count):
            e = other(k)
            arrive(hub_r.at[e, 0:rows], recv_c.at[e])

        def choose(i):
            place = jnp.full((room, D_HEAD), i, jnp.int32).astype(jnp.float32)
            chosen = hub_r[0]
            for e in range(1, count):
                chosen = jnp.where(hub_in[e, rows : rows + 1, :] == place, hub_r[e], chosen)
            return chosen

        def back(k, carry):
            i = target(k)
            hub_f[i] = choose(i)
            from_hub_back(i).start()
            return carry

        lax.fori_loop(0, count - 1, back, 0, unroll=hub_unroll)
        final[pl.ds(final_at, room), :] = choose(me)

    each_hub(lambda j: arrive(final.at[pl.ds(LEAD + room * j, rows)], recv_d.at[j]))

    square = jnp.zeros((8, D_HEAD), jnp.float32)
    mixed = []
    for h in range(heads):
        top = LEAD + room * (h // per_hub) + GROUP * (h % per_hub) - BEFORE
        got = final[top : top + 8, :] + w_v[moving, :, h * D_HEAD : (h + 1) * D_HEAD]
        square = square + got * got
        mixed.append(got)
    energy = jnp.sum(square, axis=1, keepdims=True) * (1.0 / width)
    inverse = lax.rsqrt(energy + 1e-06)
    moved = lax.broadcasted_iota(jnp.int32, (slots, D_HEAD), 0) == moving
    for h in range(heads):
        cols = slice(h * D_HEAD, (h + 1) * D_HEAD)
        row = mixed[h] * inverse * scale_v[moving, :, cols]
        for t in range(BEFORE, STEPS):
            value = jnp.where(
                moved, jnp.broadcast_to(row[t : t + 1], (slots, D_HEAD)), row_v[t, :, cols]
            )
            out_ref[t, :, cols] = value.astype(out_ref.dtype)

    each_hub(lambda j: to_hub_first(j).wait_send())
    each_hub(lambda j: to_hub_back(j).wait_send())

    @pl.when(is_hub)
    def _():
        def drain(k, carry):
            from_hub_first(other(k)).wait_send()
            from_hub_back(other(k)).wait_send()
            return carry

        lax.fori_loop(1, count, drain, 0)


def on_device(queries, keys, values, gates, states, new_slot, norm_gain):
    queries, keys, values, gates = (x.transpose(1, 0, 2) for x in (queries, keys, values, gates))
    steps, slots, width = queries.shape
    heads = states.shape[1]
    count = lax.axis_size("req")
    hubs = max(1, min(count // 2, heads // 2))
    room = -(-(GROUP * (heads // hubs) + 1) // 8) * 8
    f32, bf16 = jnp.float32, jnp.bfloat16
    hbm = pl.BlockSpec(memory_space=pl.ANY)
    dma = pltpu.SemaphoreType.DMA
    slab = pltpu.VMEM((slots, 8, width), f32)
    return pl.pallas_call(
        functools.partial(kernel, count, hubs),
        out_shape=pltpu.VMEM(queries.shape, queries.dtype),
        in_specs=[hbm] * 7,
        out_specs=pl.BlockSpec(memory_space=pltpu.VMEM),
        scratch_shapes=[
            pltpu.SMEM(new_slot.shape, new_slot.dtype),
            pltpu.VMEM(queries.shape, bf16),
            pltpu.VMEM(queries.shape, bf16),
            pltpu.VMEM(queries.shape, bf16),
            pltpu.VMEM(queries.shape, bf16),
            pltpu.VMEM((1, width), f32),
            pltpu.VMEM(states.shape, f32),
            pltpu.VMEM((slots, heads, 2 * D_HEAD, D_HEAD), bf16),
            slab,
            slab,
            slab,
            slab,
            slab,
            slab,
            pltpu.VMEM((steps, slots, width), f32),
            pltpu.VMEM((BEFORE, hubs, room, D_HEAD), f32),
            pltpu.VMEM((BEFORE, hubs, room, D_HEAD), f32),
            pltpu.VMEM((hubs, room, D_HEAD), f32),
            pltpu.VMEM((count, room, D_HEAD), f32),
            pltpu.VMEM((count, room, D_HEAD), f32),
            pltpu.VMEM((hubs, room, D_HEAD), f32),
            pltpu.VMEM((hubs, room, D_HEAD), f32),
            pltpu.VMEM((count, room, D_HEAD), f32),
            pltpu.VMEM((count, room, D_HEAD), f32),
            pltpu.VMEM((LEAD + room * hubs + 8, D_HEAD), f32),
            dma((6,)),
            dma((slots,)),
            dma((hubs,)),
            dma((count,)),
            dma((count,)),
            dma((hubs,)),
            dma((hubs,)),
            dma((count,)),
            dma((count,)),
            dma((hubs,)),
        ],
        compiler_params=pltpu.CompilerParams(collective_id=0, has_side_effects=True),
    )(new_slot, queries, keys, values, gates, norm_gain.reshape(1, width), states).transpose(
        1, 0, 2
    )


def solution(mesh):
    in_specs = (
        P(("groups", "req"), None, None),
        P(("groups", "req"), None, None),
        P(("groups", "req"), None, None),
        P(("groups", "req"), None, None),
        P(("groups", "req"), None, None, None),
        P(("groups", "req")),
        P(),
    )
    out_specs = P(("groups", "req"), None, None)
    return jax.shard_map(
        on_device, mesh=mesh, in_specs=in_specs, out_specs=out_specs, check_vma=False
    )
```

profile of v0, /device:TPU:0, one launch (start us, length us, event | category | flops | bytes accessed | tf_op | source)
XLA Modules:
  0.0 21.6 jit_solution(3232140756160079218)
XLA Ops:
  0.0 20.9 %shard_map.73 = bf16[6,2,4096]{2,1,0:T(2,128)(2,1)S(1)} custom-call(s32[2]{0:T(128)} %slot_hbm.1, bf16[6,2,4096]{2,1,0:T(2,128)(2,1)} %bitcast.7, bf16[6,2,4096]{2,1,0:T(2,128)(2,1)} %bitcast.8, bf16[6,2,4096]{2,1,0:T(2,128)(2,1)} %bitcast.9, bf16[6,2,4096]{2,1,0:T(2,128)(2,1)} %bitcast.10, f32[1,4096]{1,0:T(1,128)} %bitcast.11, f32[2,32,128,128]{3,2,1,0:T(8,128)} %s_hbm.1), custom_call_target="tpu_custom_call" | custom-call | tf_op jit(solution)/shard_map/pallas_call | solution.py:455
  20.9 0.6 %copy.9 = bf16[2,6,4096]{2,0,1:T(2,128)(2,1)} copy(bf16[2,6,4096]{2,0,1:T(2,128)(2,1)S(1)} %bitcast.6) | data formatting | bytes 196608
where the time goes:
time: 21.7 us; the launch traced here: 21.6 us
  Pallas kernels  20.9 us (96%)
  local copies, waits for them, and re-layouts  0.64 us (3%)
    pallas_call x1, Pallas kernels, on_device(): pl.pallas_call(functools.partial(kernel, count, hubs), out_shape=pltpu.VM...  20.9 us
    unnamed x1, local copies, waits for them, and re-layouts  0.64 us

commit v1 on v0

--- a/solution.py
+++ b/solution.py
@@ -90,10 +90,13 @@
     per_hub = heads // hubs
     rows = GROUP * per_hub
     room = piece.shape[1]
-    first = (count - hubs) // 2
+    first = count // 2 - hubs
     me = lax.axis_index("req")
-    is_hub = (me >= first) & (me < first + hubs)
-    hub_rank = jnp.clip(me - first, 0, hubs - 1)
+    is_hub = (me >= first) & (me < first + 2 * hubs) & (lax.rem(me, 2) == 1)
+    hub_rank = jnp.clip(me - first, 0, 2 * hubs - 1) // 2
+
+    def hub_at(j):
+        return first + 2 * j + 1
 
     loads = [
         pltpu.make_async_copy(src, dst, load_sem.at[k])
@@ -127,11 +130,6 @@
 
         lax.fori_loop(1, count, greet, 0, unroll=5 if (count - 1) % 5 == 0 else 1)
 
-    @pl.when(jnp.logical_not(is_hub))
-    def _():
-        for j in range(hubs):
-            pl.semaphore_signal(barrier, inc=1, device_id={"req": first + j}, device_id_type=MESH)
-
     for copy in loads[2:4] + state_loads + loads[4:]:
         copy.start()
 
@@ -161,7 +159,8 @@
 
     @pl.when(is_hub)
     def _():
-        pl.semaphore_wait(barrier, count - 1)
+        if hubs > 1:
+            pl.semaphore_wait(barrier, hubs - 1)
 
     @pl.when(jnp.logical_not(is_hub))
     def _():
@@ -183,7 +182,7 @@
     def each_hub(act):
         for j in range(hubs):
 
-            @pl.when(first + j != me)
+            @pl.when(hub_at(j) != me)
             def _():
                 act(j)
 
@@ -193,12 +192,12 @@
             hub_in.at[me, 0 : rows + 1],
             send_a.at[j],
             recv_a.at[me],
-            first + j,
+            hub_at(j),
         )
 
     def to_hub_back(j):
         return remote(
-            r_out.at[j, 0:rows], hub_r.at[me, 0:rows], send_c.at[j], recv_c.at[me], first + j
+            r_out.at[j, 0:rows], hub_r.at[me, 0:rows], send_c.at[j], recv_c.at[me], hub_at(j)
         )
 
     def from_hub_first(i):
@@ -221,7 +220,7 @@
     for jj in range(hubs):
         far_j = lax.rem(far + jj, hubs)
 
-        @pl.when(first + far_j != me)
+        @pl.when(hub_at(far_j) != me)
         def _():
             to_hub_first(far_j).start()
 
@@ -248,11 +247,23 @@
 
     lax.fori_loop(0, heads, halve, 0, unroll=2)
 
-    start = me - lax.rem(me, 2) + max(count // 2 - 2, 1) + count
-    own_place = lax.rem(me - start + 2 * count, count)
-
-    def target(k):
-        return lax.rem(start + k + jnp.where(k >= own_place, 1, 0), count)
+    planes = count // hubs
+    near = planes // 2 - 1
+    order = sorted(range(planes), key=lambda p: (-abs(p - near), -p))
+    own_plane = me // hubs
+    own_lane = lax.rem(me, hubs)
+
+    def far_first(k):
+        place = k // hubs
+        plane = order[-1]
+        for p in range(planes - 1):
+            plane = jnp.where(place == p, order[p], plane)
+        plane = jnp.where(own_plane == near, plane, planes - 1 - plane)
+        lane = own_lane + lax.rem(k, hubs) + jnp.where(plane == own_plane, 1, 0)
+        return plane * hubs + lax.rem(lane, hubs)
+
+    def in_turn(k):
+        return k + jnp.where(k >= me, 1, 0)
 
     hub_unroll = 5 if (count - 1) % 5 == 0 else 1
 
@@ -264,19 +275,19 @@
 
         def choose(i):
             want = hub_in[i, rows : rows + 1, :]
-            chosen = hub_in[0]
+            chosen = hub_in[0, 0:rows]
             for e in range(1, count):
-                chosen = jnp.where(want == float(e), hub_in[e], chosen)
+                chosen = jnp.where(want == float(e), hub_in[e, 0:rows], chosen)
             return chosen
 
         def hand(k, carry):
-            i = target(k)
-            hub_out[i] = choose(i)
+            i = far_first(k)
+            hub_out[i, 0:rows] = choose(i)
             from_hub_first(i).start()
             return carry
 
         lax.fori_loop(0, count - 1, hand, 0, unroll=hub_unroll)
-        q_in[hub_rank] = choose(me)
+        q_in[hub_rank, 0:rows] = choose(me)
 
     piece_row = lax.broadcasted_iota(jnp.int32, (room, D_HEAD), 0)
     piece_head = jnp.zeros((room, D_HEAD), jnp.int32)
@@ -356,7 +367,7 @@
         def others(act):
             for j in order:
 
-                @pl.when(first + j != me)
+                @pl.when(hub_at(j) != me)
                 def _():
                     act(j)
 
@@ -392,20 +403,20 @@
             arrive(hub_r.at[e, 0:rows], recv_c.at[e])
 
         def choose(i):
-            place = jnp.full((room, D_HEAD), i, jnp.int32).astype(jnp.float32)
-            chosen = hub_r[0]
+            place = jnp.full((1, D_HEAD), i, jnp.int32).astype(jnp.float32)
+            chosen = hub_r[0, 0:rows]
             for e in range(1, count):
-                chosen = jnp.where(hub_in[e, rows : rows + 1, :] == place, hub_r[e], chosen)
+                chosen = jnp.where(hub_in[e, rows : rows + 1, :] == place, hub_r[e, 0:rows], chosen)
             return chosen
 
         def back(k, carry):
-            i = target(k)
-            hub_f[i] = choose(i)
+            i = in_turn(k)
+            hub_f[i, 0:rows] = choose(i)
             from_hub_back(i).start()
             return carry
 
         lax.fori_loop(0, count - 1, back, 0, unroll=hub_unroll)
-        final[pl.ds(final_at, room), :] = choose(me)
+        final[pl.ds(final_at, rows), :] = choose(me)
 
     each_hub(lambda j: arrive(final.at[pl.ds(LEAD + room * j, rows)], recv_d.at[j]))
 
@@ -446,7 +457,7 @@
     steps, slots, width = queries.shape
     heads = states.shape[1]
     count = lax.axis_size("req")
-    hubs = max(1, min(count // 2, heads // 2))
+    hubs = max(1, min(count // 4, heads // 2))
     room = -(-(GROUP * (heads // hubs) + 1) // 8) * 8
     f32, bf16 = jnp.float32, jnp.bfloat16
     hbm = pl.BlockSpec(memory_space=pl.ANY)

time: 21.7 us -> 20.3 us (0.935)
  Pallas kernels: 20.9 us -> 19.5 us
    pallas_call x1, Pallas kernels: 20.9 us -> 19.5 us  [on_device(): pl.pallas_call(functools.partial(kernel, count, hubs), out_shape=pltpu.VM...]
where the time goes in v1:
time: 20.3 us; the launch traced here: 20.1 us
  Pallas kernels  19.5 us (96%)
  local copies, waits for them, and re-layouts  0.64 us (3%)
    pallas_call x1, Pallas kernels, on_device(): pl.pallas_call(functools.partial(kernel, count, hubs), out_shape=pltpu.VM...  19.5 us
    unnamed x1, local copies, waits for them, and re-layouts  0.64 us

profile of v1, /device:TPU:0, one launch (start us, length us, event | category | flops | bytes accessed | tf_op | source)
XLA Modules:
  0.0 20.1 jit_solution(2941902614655443442)
XLA Ops:
  0.0 19.5 %shard_map.73 = bf16[6,2,4096]{2,1,0:T(2,128)(2,1)S(1)} custom-call(s32[2]{0:T(128)} %slot_hbm.1, bf16[6,2,4096]{2,1,0:T(2,128)(2,1)} %bitcast.7, bf16[6,2,4096]{2,1,0:T(2,128)(2,1)} %bitcast.8, bf16[6,2,4096]{2,1,0:T(2,128)(2,1)} %bitcast.9, bf16[6,2,4096]{2,1,0:T(2,128)(2,1)} %bitcast.10, f32[1,4096]{1,0:T(1,128)} %bitcast.11, f32[2,32,128,128]{3,2,1,0:T(8,128)} %s_hbm.1), custom_call_target="tpu_custom_call" | custom-call | tf_op jit(solution)/shard_map/pallas_call | solution.py:466
  19.5 0.6 %copy.9 = bf16[2,6,4096]{2,0,1:T(2,128)(2,1)} copy(bf16[2,6,4096]{2,0,1:T(2,128)(2,1)S(1)} %bitcast.6) | data formatting | bytes 196608

commit v2 on v1

--- a/solution.py
+++ b/solution.py
@@ -66,6 +66,7 @@
     row_v,
     early_k,
     early_v,
+    fade,
     piece,
     hub_in,
     hub_out,
@@ -103,7 +104,8 @@
         for k, (src, dst) in enumerate(
             (
                 (slot_hbm, slot_ref),
-                (q_hbm, q_v),
+                (q_hbm.at[BEFORE:], q_v.at[BEFORE:]),
+                (q_hbm.at[:BEFORE], q_v.at[:BEFORE]),
                 (k_hbm, k_v),
                 (v_hbm, v_v),
                 (g_hbm, g_v),
@@ -130,7 +132,7 @@
 
         lax.fori_loop(1, count, greet, 0, unroll=5 if (count - 1) % 5 == 0 else 1)
 
-    for copy in loads[2:4] + state_loads + loads[4:]:
+    for copy in loads[2:5] + state_loads + loads[5:]:
         copy.start()
 
     loads[0].wait()
@@ -141,17 +143,23 @@
     wanted_row = jnp.full((1, D_HEAD), wanted, jnp.int32).astype(jnp.float32)
 
     loads[1].wait()
-    rows_of(q_v, a_v)
-    for s in range(slots):
-        a_v[s, 0:STEPS, :] = silu(a_v[s, 0:STEPS, :])
-        a_v[s, STEPS:, :] = jnp.zeros((8 - STEPS, width), jnp.float32)
-    for h in range(heads):
-        j, hh = divmod(h, per_hub)
-        piece[j, GROUP * hh : GROUP * hh + GROUP, :] = a_v[
-            moving, BEFORE:STEPS, h * D_HEAD : (h + 1) * D_HEAD
-        ]
-    for j in range(hubs):
+    span = per_hub * D_HEAD
+
+    def pack(j, carry):
+        cols = pl.ds(pl.multiple_of(j * span, D_HEAD), span)
+        for t in range(GROUP):
+            both = q_v[BEFORE + t, :, cols].astype(jnp.float32)
+            raw = both[0:1]
+            for s in range(1, slots):
+                raw = jnp.where(moving == s, both[s : s + 1], raw)
+            for hh in range(per_hub):
+                row = GROUP * hh + t
+                piece[j, row : row + 1, :] = raw[:, hh * D_HEAD : (hh + 1) * D_HEAD]
+        piece[j, 0:rows, :] = silu(piece[j, 0:rows, :])
         piece[j, rows : rows + 1, :] = wanted_row
+        return carry
+
+    lax.fori_loop(0, hubs, pack, 0)
 
     @pl.when(is_hub)
     def _():
@@ -224,9 +232,13 @@
         def _():
             to_hub_first(far_j).start()
 
-
     loads[2].wait()
+    rows_of(q_v, a_v)
+    for s in range(slots):
+        a_v[s, 0:STEPS, :] = silu(a_v[s, 0:STEPS, :])
+        a_v[s, STEPS:, :] = jnp.zeros((8 - STEPS, width), jnp.float32)
     loads[3].wait()
+    loads[4].wait()
     rows_of(k_v, b_v)
     rows_of(v_v, c_v)
     for s in range(slots):
@@ -240,12 +252,14 @@
 
     def halve(h, carry):
         for s in range(slots):
-            high, low = split(s_v[s, h])
-            s_pair[s, h, 0:D_HEAD, :] = high.astype(jnp.bfloat16)
-            s_pair[s, h, D_HEAD:, :] = low.astype(jnp.bfloat16)
+            for side in range(2):
+                cols = slice(side * D_HEAD, (side + 1) * D_HEAD)
+                high, low = split(s_v[s, 2 * h + side])
+                s_pair[s, h, 0:D_HEAD, cols] = high.astype(jnp.bfloat16)
+                s_pair[s, h, D_HEAD:, cols] = low.astype(jnp.bfloat16)
         return carry
 
-    lax.fori_loop(0, heads, halve, 0, unroll=2)
+    lax.fori_loop(0, heads // 2, halve, 0)
 
     planes = count // hubs
     near = planes // 2 - 1
@@ -269,9 +283,11 @@
 
     @pl.when(is_hub)
     def _():
-        for k in range(1, count):
-            e = other(k)
-            arrive(hub_in.at[e, 0 : rows + 1], recv_a.at[e])
+        def gather(k, carry):
+            arrive(hub_in.at[other(k), 0 : rows + 1], recv_a.at[other(k)])
+            return carry
+
+        lax.fori_loop(1, count, gather, 0)
 
         def choose(i):
             want = hub_in[i, rows : rows + 1, :]
@@ -289,11 +305,19 @@
         lax.fori_loop(0, count - 1, hand, 0, unroll=hub_unroll)
         q_in[hub_rank, 0:rows] = choose(me)
 
-    piece_row = lax.broadcasted_iota(jnp.int32, (room, D_HEAD), 0)
-    piece_head = jnp.zeros((room, D_HEAD), jnp.int32)
+    piece_row = lax.broadcasted_iota(jnp.int32, (rows, D_HEAD), 0)
+    piece_head = jnp.zeros((rows, D_HEAD), jnp.int32)
     for hh in range(1, per_hub):
         piece_head = jnp.where(piece_row >= GROUP * hh, hh, piece_head)
     piece_step = (piece_row - GROUP * piece_head).astype(jnp.float32)
+    def fading(j, carry):
+        slope = head_slope((piece_head + j * per_hub).astype(jnp.float32))
+        fade[j, 0] = jnp.exp(-slope * (piece_step + (BEFORE + 1.0)))
+        for s in range(BEFORE):
+            fade[j, 1 + s] = jnp.exp(-slope * (piece_step + float(BEFORE - s)))
+        return carry
+
+    lax.fori_loop(0, hubs, fading, 0)
     for h in range(heads):
         j, hh = divmod(h, per_hub)
         cols = slice(h * D_HEAD, (h + 1) * D_HEAD)
@@ -308,80 +332,90 @@
     step = lax.broadcasted_iota(jnp.int32, (8, D_HEAD), 0)
     step_f = step.astype(jnp.float32)
 
-    def own(h, carry):
-        cols = pl.ds(pl.multiple_of(h * D_HEAD, D_HEAD), D_HEAD)
-        slope = head_slope(jnp.full((8, D_HEAD), h, jnp.int32).astype(jnp.float32))
-        decay_state = jnp.exp(-slope * (step_f + 1.0))
+    def own(pair, carry):
         for s in range(slots):
-            a, b, c = a_v[s, :, cols], b_v[s, :, cols], c_v[s, :, cols]
-            high, low = split(a)
-            left = jnp.concatenate([high, low], axis=0)
-            left = jnp.concatenate([left, left], axis=1).astype(jnp.bfloat16)
-            both = jnp.dot(left, s_pair[s, h], preferred_element_type=jnp.float32)
-            base = decay_state * (both[:8] + both[8:])
-            within = jnp.zeros((8, D_HEAD), jnp.float32)
-            for back in range(STEPS):
-                b_back = pltpu.roll(b, back, 0) if back else b
-                c_back = pltpu.roll(c, back, 0) if back else c
-                mix = jnp.sum(a * b_back, axis=1, keepdims=True)
-                term = mix * c_back * jnp.exp(-slope * float(back))
-                late = (step >= BEFORE) & (step < STEPS)
-                if back < BEFORE:
-                    keep = ((step < BEFORE) & (step >= back)) | (late & (step >= BEFORE + back))
-                    within = within + jnp.where(keep, term, 0.0)
-                if back:
-                    cross = late & (step >= back) & (step < BEFORE + back)
-                    base = base + jnp.where(cross, term, 0.0)
-            base_v[s, :, cols] = base
-            w_v[s, :, cols] = within
+            wide = pl.ds(pl.multiple_of(pair * 2 * D_HEAD, D_HEAD), 2 * D_HEAD)
+            a_high, a_low = split(a_v[s, :, wide])
+            for side in range(2):
+                h = 2 * pair + side
+                here = slice(side * D_HEAD, (side + 1) * D_HEAD)
+                cols = pl.ds(pl.multiple_of(h * D_HEAD, D_HEAD), D_HEAD)
+                slope = head_slope(jnp.full((8, D_HEAD), h, jnp.int32).astype(jnp.float32))
+                decay_state = jnp.exp(-slope * (step_f + 1.0))
+                a, b, c = a_v[s, :, cols], b_v[s, :, cols], c_v[s, :, cols]
+                left = jnp.concatenate([a_high[:, here], a_low[:, here]], axis=0)
+                left = jnp.concatenate([left, left], axis=1).astype(jnp.bfloat16)
+                both = jnp.dot(
+                    left, s_pair[s, pair, :, here], preferred_element_type=jnp.float32
+                )
+                base = decay_state * (both[:8] + both[8:])
+                within = jnp.zeros((8, D_HEAD), jnp.float32)
+                for back in range(STEPS):
+                    b_back = pltpu.roll(b, back, 0) if back else b
+                    c_back = pltpu.roll(c, back, 0) if back else c
+                    mix = jnp.sum(a * b_back, axis=1, keepdims=True)
+                    term = mix * c_back * jnp.exp(-slope * float(back))
+                    late = (step >= BEFORE) & (step < STEPS)
+                    if back < BEFORE:
+                        keep = ((step < BEFORE) & (step >= back)) | (late & (step >= BEFORE + back))
+                        within = within + jnp.where(keep, term, 0.0)
+                    if back:
+                        cross = late & (step >= back) & (step < BEFORE + back)
+                        base = base + jnp.where(cross, term, 0.0)
+                base_v[s, :, cols] = base
+                w_v[s, :, cols] = within
         return carry
 
-    lax.fori_loop(0, heads, own, 0, unroll=2)
+    lax.fori_loop(0, heads // 2, own, 0)
 
     def answer(j):
-        q = q_in[j]
+        q = q_in[j, 0:rows]
         high, low = split(q)
         left = jnp.concatenate([high, low], axis=0)
         left = jnp.concatenate([left, left], axis=1).astype(jnp.bfloat16)
-        slope = head_slope((piece_head + j * per_hub).astype(jnp.float32))
-        total = jnp.zeros((room, D_HEAD), jnp.float32)
-        for hh in range(per_hub):
+        total = jnp.zeros((rows, D_HEAD), jnp.float32)
+        for pair in range(per_hub // 2):
             both = jnp.dot(
-                left, s_pair[moving, j * per_hub + hh], preferred_element_type=jnp.float32
+                left, s_pair[moving, j * (per_hub // 2) + pair], preferred_element_type=jnp.float32
             )
-            total = jnp.where(piece_head == hh, both[:room] + both[room:], total)
-        total = total * jnp.exp(-slope * (piece_step + (BEFORE + 1.0)))
+            both = both[:rows] + both[rows:]
+            for side in range(2):
+                total = jnp.where(
+                    piece_head == 2 * pair + side,
+                    both[:, side * D_HEAD : (side + 1) * D_HEAD],
+                    total,
+                )
+        total = total * fade[j, 0]
         for s in range(BEFORE):
-            mix = jnp.sum(q * early_k[s, j], axis=1, keepdims=True)
-            total = total + mix * early_v[s, j] * jnp.exp(
-                -slope * (piece_step + float(BEFORE - s))
-            )
-        r_out[j] = total
-
-    split_at = max(1, hubs // 2)
-    turn = jnp.where(me >= count // 2, split_at, 0)
-    share = max(1, hubs // 4)
-    for group in [range(k, min(k + share, hubs)) for k in range(0, hubs, share)]:
-        order = [lax.rem(turn + jj, hubs) for jj in group]
-
-        def others(act):
-            for j in order:
-
-                @pl.when(hub_at(j) != me)
-                def _():
-                    act(j)
-
-        others(lambda j: arrive(q_in.at[j, 0:rows], recv_b.at[j]))
-        for j in order:
-            answer(j)
-        others(lambda j: to_hub_back(j).start())
+            mix = jnp.sum(q * early_k[s, j, 0:rows], axis=1, keepdims=True)
+            total = total + mix * early_v[s, j, 0:rows] * fade[j, 1 + s]
+        r_out[j, 0:rows] = total
+
+    turn = jnp.where(me >= count // 2, max(1, hubs // 2), 0)
+
+    def reply(jj, carry):
+        j = lax.rem(turn + jj, hubs)
+
+        @pl.when(hub_at(j) != me)
+        def _():
+            arrive(q_in.at[j, 0:rows], recv_b.at[j])
+
+        answer(j)
+
+        @pl.when(hub_at(j) != me)
+        def _():
+            to_hub_back(j).start()
+
+        return carry
+
+    lax.fori_loop(0, hubs, reply, 0)
 
     @pl.when(is_hub)
     def _():
         hub_r[me] = r_out[hub_rank]
 
-    loads[4].wait()
     loads[5].wait()
+    loads[6].wait()
     rows_of(g_v, scale_v)
     for s in range(slots):
         gate = scale_v[s, 0:STEPS, :]
@@ -398,9 +432,11 @@
 
     @pl.when(is_hub)
     def _():
-        for k in range(1, count):
-            e = other(k)
-            arrive(hub_r.at[e, 0:rows], recv_c.at[e])
+        def gather(k, carry):
+            arrive(hub_r.at[other(k), 0:rows], recv_c.at[other(k)])
+            return carry
+
+        lax.fori_loop(1, count, gather, 0)
 
         def choose(i):
             place = jnp.full((1, D_HEAD), i, jnp.int32).astype(jnp.float32)
@@ -417,6 +453,9 @@
 
         lax.fori_loop(0, count - 1, back, 0, unroll=hub_unroll)
         final[pl.ds(final_at, rows), :] = choose(me)
+
+    each_hub(lambda j: to_hub_first(j).wait_send())
+    each_hub(lambda j: to_hub_back(j).wait_send())
 
     each_hub(lambda j: arrive(final.at[pl.ds(LEAD + room * j, rows)], recv_d.at[j]))
 
@@ -438,9 +477,6 @@
                 moved, jnp.broadcast_to(row[t : t + 1], (slots, D_HEAD)), row_v[t, :, cols]
             )
             out_ref[t, :, cols] = value.astype(out_ref.dtype)
-
-    each_hub(lambda j: to_hub_first(j).wait_send())
-    each_hub(lambda j: to_hub_back(j).wait_send())
 
     @pl.when(is_hub)
     def _():
@@ -476,7 +512,7 @@
             pltpu.VMEM(queries.shape, bf16),
             pltpu.VMEM((1, width), f32),
             pltpu.VMEM(states.shape, f32),
-            pltpu.VMEM((slots, heads, 2 * D_HEAD, D_HEAD), bf16),
+            pltpu.VMEM((slots, heads // 2, 2 * D_HEAD, 2 * D_HEAD), bf16),
             slab,
             slab,
             slab,
@@ -486,6 +522,7 @@
             pltpu.VMEM((steps, slots, width), f32),
             pltpu.VMEM((BEFORE, hubs, room, D_HEAD), f32),
             pltpu.VMEM((BEFORE, hubs, room, D_HEAD), f32),
+            pltpu.VMEM((hubs, 1 + BEFORE, GROUP * (heads // hubs), D_HEAD), f32),
             pltpu.VMEM((hubs, room, D_HEAD), f32),
             pltpu.VMEM((count, room, D_HEAD), f32),
             pltpu.VMEM((count, room, D_HEAD), f32),
@@ -494,7 +531,7 @@
             pltpu.VMEM((count, room, D_HEAD), f32),
             pltpu.VMEM((count, room, D_HEAD), f32),
             pltpu.VMEM((LEAD + room * hubs + 8, D_HEAD), f32),
-            dma((6,)),
+            dma((7,)),
             dma((slots,)),
             dma((hubs,)),
             dma((count,)),

time: 20.3 us -> 20.1 us (level)
  no operation moved by 1% of the time
where the time goes in v2:
time: 20.1 us; the launch traced here: 20 us
  Pallas kernels  19.3 us (96%)
  local copies, waits for them, and re-layouts  0.64 us (3%)
    pallas_call x1, Pallas kernels, on_device(): pl.pallas_call(functools.partial(kernel, count, hubs), out_shape=pltpu.VM...  19.3 us
    unnamed x1, local copies, waits for them, and re-layouts  0.64 us

profile of v2, /device:TPU:0, one launch (start us, length us, event | category | flops | bytes accessed | tf_op | source)
XLA Modules:
  0.0 20.0 jit_solution(7769622547217409095)
XLA Ops:
  0.0 19.3 %shard_map.73 = bf16[6,2,4096]{2,1,0:T(2,128)(2,1)S(1)} custom-call(s32[2]{0:T(128)} %slot_hbm.1, bf16[6,2,4096]{2,1,0:T(2,128)(2,1)} %bitcast.7, bf16[6,2,4096]{2,1,0:T(2,128)(2,1)} %bitcast.8, bf16[6,2,4096]{2,1,0:T(2,128)(2,1)} %bitcast.9, bf16[6,2,4096]{2,1,0:T(2,128)(2,1)} %bitcast.10, f32[1,4096]{1,0:T(1,128)} %bitcast.11, f32[2,32,128,128]{3,2,1,0:T(8,128)} %s_hbm.1), custom_call_target="tpu_custom_call" | custom-call | tf_op jit(solution)/shard_map/pallas_call | solution.py:502
  19.4 0.6 %copy.9 = bf16[2,6,4096]{2,0,1:T(2,128)(2,1)} copy(bf16[2,6,4096]{2,0,1:T(2,128)(2,1)S(1)} %bitcast.6) | data formatting | bytes 196608

commit v3 on v2

--- a/solution.py
+++ b/solution.py
@@ -91,6 +91,7 @@
     per_hub = heads // hubs
     rows = GROUP * per_hub
     room = piece.shape[1]
+    full = fade.shape[2]
     first = count // 2 - hubs
     me = lax.axis_index("req")
     is_hub = (me >= first) & (me < first + 2 * hubs) & (lax.rem(me, 2) == 1)
@@ -305,8 +306,8 @@
         lax.fori_loop(0, count - 1, hand, 0, unroll=hub_unroll)
         q_in[hub_rank, 0:rows] = choose(me)
 
-    piece_row = lax.broadcasted_iota(jnp.int32, (rows, D_HEAD), 0)
-    piece_head = jnp.zeros((rows, D_HEAD), jnp.int32)
+    piece_row = lax.broadcasted_iota(jnp.int32, (full, D_HEAD), 0)
+    piece_head = jnp.zeros((full, D_HEAD), jnp.int32)
     for hh in range(1, per_hub):
         piece_head = jnp.where(piece_row >= GROUP * hh, hh, piece_head)
     piece_step = (piece_row - GROUP * piece_head).astype(jnp.float32)
@@ -332,83 +333,107 @@
     step = lax.broadcasted_iota(jnp.int32, (8, D_HEAD), 0)
     step_f = step.astype(jnp.float32)
 
-    def own(pair, carry):
-        for s in range(slots):
-            wide = pl.ds(pl.multiple_of(pair * 2 * D_HEAD, D_HEAD), 2 * D_HEAD)
-            a_high, a_low = split(a_v[s, :, wide])
-            for side in range(2):
-                h = 2 * pair + side
-                here = slice(side * D_HEAD, (side + 1) * D_HEAD)
-                cols = pl.ds(pl.multiple_of(h * D_HEAD, D_HEAD), D_HEAD)
-                slope = head_slope(jnp.full((8, D_HEAD), h, jnp.int32).astype(jnp.float32))
-                decay_state = jnp.exp(-slope * (step_f + 1.0))
-                a, b, c = a_v[s, :, cols], b_v[s, :, cols], c_v[s, :, cols]
-                left = jnp.concatenate([a_high[:, here], a_low[:, here]], axis=0)
+    def owns(*parts):
+        def own(pair, carry):
+            for s in range(slots):
+                wide = pl.ds(pl.multiple_of(pair * 2 * D_HEAD, D_HEAD), 2 * D_HEAD)
+                a_high, a_low = split(a_v[s, :, wide])
+                left = jnp.concatenate(
+                    [x[:, k * D_HEAD : (k + 1) * D_HEAD] for k in range(2) for x in (a_high, a_low)],
+                    axis=0,
+                )
                 left = jnp.concatenate([left, left], axis=1).astype(jnp.bfloat16)
-                both = jnp.dot(
-                    left, s_pair[s, pair, :, here], preferred_element_type=jnp.float32
-                )
-                base = decay_state * (both[:8] + both[8:])
-                within = jnp.zeros((8, D_HEAD), jnp.float32)
-                for back in range(STEPS):
-                    b_back = pltpu.roll(b, back, 0) if back else b
-                    c_back = pltpu.roll(c, back, 0) if back else c
-                    mix = jnp.sum(a * b_back, axis=1, keepdims=True)
-                    term = mix * c_back * jnp.exp(-slope * float(back))
-                    late = (step >= BEFORE) & (step < STEPS)
-                    if back < BEFORE:
-                        keep = ((step < BEFORE) & (step >= back)) | (late & (step >= BEFORE + back))
-                        within = within + jnp.where(keep, term, 0.0)
-                    if back:
-                        cross = late & (step >= back) & (step < BEFORE + back)
-                        base = base + jnp.where(cross, term, 0.0)
-                base_v[s, :, cols] = base
-                w_v[s, :, cols] = within
-        return carry
-
-    lax.fori_loop(0, heads // 2, own, 0)
-
-    def answer(j):
-        q = q_in[j, 0:rows]
-        high, low = split(q)
-        left = jnp.concatenate([high, low], axis=0)
-        left = jnp.concatenate([left, left], axis=1).astype(jnp.bfloat16)
-        total = jnp.zeros((rows, D_HEAD), jnp.float32)
-        for pair in range(per_hub // 2):
-            both = jnp.dot(
-                left, s_pair[moving, j * (per_hub // 2) + pair], preferred_element_type=jnp.float32
-            )
-            both = both[:rows] + both[rows:]
-            for side in range(2):
-                total = jnp.where(
-                    piece_head == 2 * pair + side,
-                    both[:, side * D_HEAD : (side + 1) * D_HEAD],
-                    total,
-                )
-        total = total * fade[j, 0]
-        for s in range(BEFORE):
-            mix = jnp.sum(q * early_k[s, j, 0:rows], axis=1, keepdims=True)
-            total = total + mix * early_v[s, j, 0:rows] * fade[j, 1 + s]
-        r_out[j, 0:rows] = total
-
-    turn = jnp.where(me >= count // 2, max(1, hubs // 2), 0)
-
-    def reply(jj, carry):
-        j = lax.rem(turn + jj, hubs)
-
-        @pl.when(hub_at(j) != me)
-        def _():
-            arrive(q_in.at[j, 0:rows], recv_b.at[j])
-
-        answer(j)
-
-        @pl.when(hub_at(j) != me)
-        def _():
-            to_hub_back(j).start()
-
-        return carry
-
-    lax.fori_loop(0, hubs, reply, 0)
+                pltpu.matmul_push_rhs(s_pair[s, pair], 0, s % 2)
+                pltpu.matmul_acc_lhs(parts[s % 2], left, load_staged_rhs=0)
+                product = pltpu.matmul_pop(parts[s % 2])
+                for side in range(2):
+                    h = 2 * pair + side
+                    here = slice(side * D_HEAD, (side + 1) * D_HEAD)
+                    cols = pl.ds(pl.multiple_of(h * D_HEAD, D_HEAD), D_HEAD)
+                    slope = head_slope(jnp.full((8, D_HEAD), h, jnp.int32).astype(jnp.float32))
+                    decay_state = jnp.exp(-slope * (step_f + 1.0))
+                    a, b, c = a_v[s, :, cols], b_v[s, :, cols], c_v[s, :, cols]
+                    both = product[16 * side : 16 * (side + 1), here]
+                    base = decay_state * (both[:8] + both[8:])
+                    within = jnp.zeros((8, D_HEAD), jnp.float32)
+                    for back in range(STEPS):
+                        b_back = pltpu.roll(b, back, 0) if back else b
+                        c_back = pltpu.roll(c, back, 0) if back else c
+                        mix = jnp.sum(a * b_back, axis=1, keepdims=True)
+                        term = mix * c_back * jnp.exp(-slope * float(back))
+                        late = (step >= BEFORE) & (step < STEPS)
+                        if back < BEFORE:
+                            keep = ((step < BEFORE) & (step >= back)) | (late & (step >= BEFORE + back))
+                            within = within + jnp.where(keep, term, 0.0)
+                        if back:
+                            cross = late & (step >= back) & (step < BEFORE + back)
+                            base = base + jnp.where(cross, term, 0.0)
+                    base_v[s, :, cols] = base
+                    w_v[s, :, cols] = within
+            return carry
+
+        lax.fori_loop(0, heads // 2, own, 0)
+
+    pl.run_scoped(owns, *(pltpu.ACC(mxu_id=k)((32, 2 * D_HEAD), jnp.float32) for k in range(2)))
+
+    pairs = per_hub // 2
+    staged = min(4, pairs)
+
+    def stage(j, begin):
+        for k in range(min(staged, pairs - begin)):
+            pltpu.matmul_push_rhs(s_pair[moving, j * pairs + begin + k], k // 2, k % 2)
+
+    def replies(*sums):
+        def answer(j):
+            q = q_in[j, 0:full]
+            high, low = split(q)
+            left = jnp.concatenate([high, low], axis=0)
+            left = jnp.concatenate([left, left], axis=1).astype(jnp.bfloat16)
+            total = jnp.zeros((full, D_HEAD), jnp.float32)
+            for begin in range(0, pairs, staged):
+                if begin:
+                    stage(j, begin)
+                for k in range(min(staged, pairs - begin)):
+                    pltpu.matmul_acc_lhs(sums[k], left, load_staged_rhs=k // 2)
+                for k in range(min(staged, pairs - begin)):
+                    both = pltpu.matmul_pop(sums[k])
+                    both = both[:full] + both[full:]
+                    for side in range(2):
+                        total = jnp.where(
+                            piece_head == 2 * (begin + k) + side,
+                            both[:, side * D_HEAD : (side + 1) * D_HEAD],
+                            total,
+                        )
+            total = total * fade[j, 0]
+            for s in range(BEFORE):
+                mix = jnp.sum(q * early_k[s, j, 0:full], axis=1, keepdims=True)
+                total = total + mix * early_v[s, j, 0:full] * fade[j, 1 + s]
+            r_out[j, 0:full] = total
+
+        turn = jnp.where(me >= count // 2, max(1, hubs // 2), 0)
+
+        def reply(jj, carry):
+            j = lax.rem(turn + jj, hubs)
+            stage(j, 0)
+
+            @pl.when(hub_at(j) != me)
+            def _():
+                arrive(q_in.at[j, 0:rows], recv_b.at[j])
+
+            answer(j)
+
+            @pl.when(hub_at(j) != me)
+            def _():
+                to_hub_back(j).start()
+
+            return carry
+
+        lax.fori_loop(0, hubs, reply, 0)
+
+    pl.run_scoped(
+        replies,
+        *(pltpu.ACC(mxu_id=k % 2)((2 * full, 2 * D_HEAD), jnp.float32) for k in range(staged)),
+    )
 
     @pl.when(is_hub)
     def _():
@@ -522,7 +547,7 @@
             pltpu.VMEM((steps, slots, width), f32),
             pltpu.VMEM((BEFORE, hubs, room, D_HEAD), f32),
             pltpu.VMEM((BEFORE, hubs, room, D_HEAD), f32),
-            pltpu.VMEM((hubs, 1 + BEFORE, GROUP * (heads // hubs), D_HEAD), f32),
+            pltpu.VMEM((hubs, 1 + BEFORE, -(-GROUP * (heads // hubs) // 8) * 8, D_HEAD), f32),
             pltpu.VMEM((hubs, room, D_HEAD), f32),
             pltpu.VMEM((count, room, D_HEAD), f32),
             pltpu.VMEM((count, room, D_HEAD), f32),

time: 20.1 us -> 20.1 us (level)
  no operation moved by 1% of the time
where the time goes in v3:
time: 20.1 us; the launch traced here: 20 us
  Pallas kernels  19.3 us (96%)
  local copies, waits for them, and re-layouts  0.64 us (3%)
    pallas_call x1, Pallas kernels, on_device(): pl.pallas_call(functools.partial(kernel, count, hubs), out_shape=pltpu.VM...  19.3 us
    unnamed x1, local copies, waits for them, and re-layouts  0.64 us

profile of v3, /device:TPU:0, one launch (start us, length us, event | category | flops | bytes accessed | tf_op | source)
XLA Modules:
  0.0 20.0 jit_solution(13080735773170584499)
XLA Ops:
  0.0 19.3 %shard_map.73 = bf16[6,2,4096]{2,1,0:T(2,128)(2,1)S(1)} custom-call(s32[2]{0:T(128)} %slot_hbm.1, bf16[6,2,4096]{2,1,0:T(2,128)(2,1)} %bitcast.7, bf16[6,2,4096]{2,1,0:T(2,128)(2,1)} %bitcast.8, bf16[6,2,4096]{2,1,0:T(2,128)(2,1)} %bitcast.9, bf16[6,2,4096]{2,1,0:T(2,128)(2,1)} %bitcast.10, f32[1,4096]{1,0:T(1,128)} %bitcast.11, f32[2,32,128,128]{3,2,1,0:T(8,128)} %s_hbm.1), custom_call_target="tpu_custom_call" | custom-call | tf_op jit(solution)/shard_map/pallas_call | solution.py:527
  19.3 0.6 %copy.9 = bf16[2,6,4096]{2,0,1:T(2,128)(2,1)} copy(bf16[2,6,4096]{2,0,1:T(2,128)(2,1)S(1)} %bitcast.6) | data formatting | bytes 196608

commit v4 on v3

--- a/solution.py
+++ b/solution.py
@@ -298,7 +298,7 @@
             return chosen
 
         def hand(k, carry):
-            i = far_first(k)
+            i = jnp.where(own_plane == near, count - 1 - (k + jnp.where(k >= count - 1 - me, 1, 0)), in_turn(k))
             hub_out[i, 0:rows] = choose(i)
             from_hub_first(i).start()
             return carry
@@ -410,7 +410,7 @@
                 total = total + mix * early_v[s, j, 0:full] * fade[j, 1 + s]
             r_out[j, 0:full] = total
 
-        turn = jnp.where(me >= count // 2, max(1, hubs // 2), 0)
+        turn = jnp.where(me >= count // 2, 0, max(1, hubs // 2))
 
         def reply(jj, carry):
             j = lax.rem(turn + jj, hubs)

time: 20.1 us -> 19.6 us (0.975)
  Pallas kernels: 19.3 us -> 18.8 us
    pallas_call x1, Pallas kernels: 19.3 us -> 18.8 us  [on_device(): pl.pallas_call(functools.partial(kernel, count, hubs), out_shape=pltpu.VM...]
where the time goes in v4:
time: 19.6 us; the launch traced here: 19.4 us
  Pallas kernels  18.8 us (96%)
  local copies, waits for them, and re-layouts  0.64 us (3%)
    pallas_call x1, Pallas kernels, on_device(): pl.pallas_call(functools.partial(kernel, count, hubs), out_shape=pltpu.VM...  18.8 us
    unnamed x1, local copies, waits for them, and re-layouts  0.64 us

profile of v4, /device:TPU:0, one launch (start us, length us, event | category | flops | bytes accessed | tf_op | source)
XLA Modules:
  0.0 19.4 jit_solution(4450021288645646406)
XLA Ops:
  0.0 18.8 %shard_map.73 = bf16[6,2,4096]{2,1,0:T(2,128)(2,1)S(1)} custom-call(s32[2]{0:T(128)} %slot_hbm.1, bf16[6,2,4096]{2,1,0:T(2,128)(2,1)} %bitcast.7, bf16[6,2,4096]{2,1,0:T(2,128)(2,1)} %bitcast.8, bf16[6,2,4096]{2,1,0:T(2,128)(2,1)} %bitcast.9, bf16[6,2,4096]{2,1,0:T(2,128)(2,1)} %bitcast.10, f32[1,4096]{1,0:T(1,128)} %bitcast.11, f32[2,32,128,128]{3,2,1,0:T(8,128)} %s_hbm.1), custom_call_target="tpu_custom_call" | custom-call | tf_op jit(solution)/shard_map/pallas_call | solution.py:527
  18.8 0.6 %copy.9 = bf16[2,6,4096]{2,0,1:T(2,128)(2,1)} copy(bf16[2,6,4096]{2,0,1:T(2,128)(2,1)S(1)} %bitcast.6) | data formatting | bytes 196608

commit v5 on v4

--- a/solution.py
+++ b/solution.py
@@ -280,7 +280,7 @@
     def in_turn(k):
         return k + jnp.where(k >= me, 1, 0)
 
-    hub_unroll = 5 if (count - 1) % 5 == 0 else 1
+    hub_unroll = 3
 
     @pl.when(is_hub)
     def _():
@@ -413,7 +413,7 @@
         turn = jnp.where(me >= count // 2, 0, max(1, hubs // 2))
 
         def reply(jj, carry):
-            j = lax.rem(turn + jj, hubs)
+            j = jnp.where(me >= count // 2, jj, hubs - 1 - jj)
             stage(j, 0)
 
             @pl.when(hub_at(j) != me)

time: 19.6 us -> 19.6 us (level)
  no operation moved by 1% of the time
where the time goes in v5:
time: 19.6 us; the launch traced here: 19.4 us
  Pallas kernels  18.8 us (96%)
  local copies, waits for them, and re-layouts  0.64 us (3%)
    pallas_call x1, Pallas kernels, on_device(): pl.pallas_call(functools.partial(kernel, count, hubs), out_shape=pltpu.VM...  18.8 us
    unnamed x1, local copies, waits for them, and re-layouts  0.64 us

profile of v5, /device:TPU:0, one launch (start us, length us, event | category | flops | bytes accessed | tf_op | source)
XLA Modules:
  0.0 19.4 jit_solution(12825825043509706622)
XLA Ops:
  0.0 18.8 %shard_map.73 = bf16[6,2,4096]{2,1,0:T(2,128)(2,1)S(1)} custom-call(s32[2]{0:T(128)} %slot_hbm.1, bf16[6,2,4096]{2,1,0:T(2,128)(2,1)} %bitcast.7, bf16[6,2,4096]{2,1,0:T(2,128)(2,1)} %bitcast.8, bf16[6,2,4096]{2,1,0:T(2,128)(2,1)} %bitcast.9, bf16[6,2,4096]{2,1,0:T(2,128)(2,1)} %bitcast.10, f32[1,4096]{1,0:T(1,128)} %bitcast.11, f32[2,32,128,128]{3,2,1,0:T(8,128)} %s_hbm.1), custom_call_target="tpu_custom_call" | custom-call | tf_op jit(solution)/shard_map/pallas_call | solution.py:527
  18.8 0.6 %copy.9 = bf16[2,6,4096]{2,0,1:T(2,128)(2,1)} copy(bf16[2,6,4096]{2,0,1:T(2,128)(2,1)S(1)} %bitcast.6) | data formatting | bytes 196608

commit v6 on v4

--- a/solution.py
+++ b/solution.py
@@ -227,7 +227,7 @@
 
     far = jnp.where(me >= count // 2, 0, max(1, hubs // 2))
     for jj in range(hubs):
-        far_j = lax.rem(far + jj, hubs)
+        far_j = jnp.where(me >= count // 2, jj, hubs - 1 - jj)
 
         @pl.when(hub_at(far_j) != me)
         def _():

time: 19.6 us -> 19.5 us (level)
  no operation moved by 1% of the time
where the time goes in v6:
time: 19.5 us; the launch traced here: 19.4 us
  Pallas kernels  18.7 us (96%)
  local copies, waits for them, and re-layouts  0.64 us (3%)
    pallas_call x1, Pallas kernels, on_device(): pl.pallas_call(functools.partial(kernel, count, hubs), out_shape=pltpu.VM...  18.7 us
    unnamed x1, local copies, waits for them, and re-layouts  0.64 us

profile of v6, /device:TPU:0, one launch (start us, length us, event | category | flops | bytes accessed | tf_op | source)
XLA Modules:
  0.0 19.4 jit_solution(8537226784500874711)
XLA Ops:
  0.0 18.7 %shard_map.73 = bf16[6,2,4096]{2,1,0:T(2,128)(2,1)S(1)} custom-call(s32[2]{0:T(128)} %slot_hbm.1, bf16[6,2,4096]{2,1,0:T(2,128)(2,1)} %bitcast.7, bf16[6,2,4096]{2,1,0:T(2,128)(2,1)} %bitcast.8, bf16[6,2,4096]{2,1,0:T(2,128)(2,1)} %bitcast.9, bf16[6,2,4096]{2,1,0:T(2,128)(2,1)} %bitcast.10, f32[1,4096]{1,0:T(1,128)} %bitcast.11, f32[2,32,128,128]{3,2,1,0:T(8,128)} %s_hbm.1), custom_call_target="tpu_custom_call" | custom-call | tf_op jit(solution)/shard_map/pallas_call | solution.py:527
  18.8 0.6 %copy.9 = bf16[2,6,4096]{2,0,1:T(2,128)(2,1)} copy(bf16[2,6,4096]{2,0,1:T(2,128)(2,1)S(1)} %bitcast.6) | data formatting | bytes 196608
